TPU v7x, 32 devices: a whole 2x2x4 slice. The times are simulated.
32 devices in a mesh: shard: 4 (over z), tensor: 2 (over core), section: 4 (over y, x).
Axes of the slice: x: 2, y: 2, z: 4, core: 2. Of those that a mesh axis runs over, the one named last changes fastest.
Arguments:
- gradient: bfloat16 [2560, 2560], P('shard', ('tensor', 'section')), may hold values from -100 to 100
- gain_grad: float32 [2, 2560], P(None, 'shard'), may hold values from -12 to 12
- left_statistic: float32 [2560, 2560], P('shard', ('tensor', 'section')), may hold values from -1 to 3, as said below
- left_basis: float32 [2560, 2560], P('shard', ('tensor', 'section')), may hold values from -1 to 1.5
- first_moment: float32 [2560, 2560], P('shard', ('tensor', 'section')), may hold values from -3 to 3
- second_moment: float32 [2560, 2560], P('shard', ('tensor', 'section')), may hold values from 0.2 to 2
- norm_gains: float32 [2, 2560], P(None, 'shard'), may hold values from 0.5 to 1.5
- gain_first: float32 [2, 2560], P(None, 'shard'), may hold values from -2 to 2
- gain_second: float32 [2, 2560], P(None, 'shard'), may hold values from 0.5 to 5
Outputs:
- update: float32 [2560, 2560], P('shard', ('tensor', 'section'))
- new_first: float32 [2560, 2560], P('shard', ('tensor', 'section'))
- new_second: float32 [2560, 2560], P('shard', ('tensor', 'section'))
- new_statistic: float32 [2560, 2560], P('shard', ('tensor', 'section'))
- new_basis: float32 [2560, 2560], P('shard', ('tensor', 'section'))
- new_gains: float32 [2, 2560], P(None, 'shard')
- new_gain_first: float32 [2, 2560], P(None, 'shard')
- new_gain_second: float32 [2, 2560], P(None, 'shard')
Inputs may be any that keep to these rules, and one draw needn't show every extreme that they name: `left_statistic`: symmetric.
All inputs are finite; a program needn't handle non-finite values.
Results may differ from a plain program's by a relative error of at most 0.0003.
Values may be sent and summed in bfloat16 or wider, within the bound.
A program may use at most 128 MiB of HBM per device.

v0:
```python
import jax
import jax.numpy as jnp
from jax import lax
from jax.sharding import PartitionSpec as P

D = 2560
NS_STEPS = 3
GROUP = ("tensor", "section")
EVERY = ("shard", "tensor", "section")
PAD = 16


def matmul(left_side, right_side):
    return jnp.dot(
        left_side, right_side, precision=lax.Precision.HIGH, preferred_element_type=jnp.float32
    )


def row_panel(local_block):
    return lax.all_gather(local_block, GROUP, axis=1, tiled=True)


def same(block):
    return block


def pack(block):
    top = jnp.max(jnp.abs(block), axis=0, keepdims=True)
    power = jnp.clip(jnp.ceil(jnp.log2(jnp.maximum(top, 1e-30))) - 14.0, -110.0, 120.0)
    scaled = block * jnp.exp2(-power)
    tail = jnp.broadcast_to(power, (PAD, block.shape[1]))
    return jnp.concatenate([scaled, tail], axis=0).astype(jnp.float16)


def unpack(payload):
    values = payload.astype(jnp.float32)
    return values[..., :-PAD, :] * jnp.exp2(values[..., -PAD : -PAD + 1, :])


def partners(size):
    if size & size - 1 == 0:
        return [[(one, one ^ offset) for one in range(size)] for offset in range(1, size)]
    return [[(one, (one + offset) % size) for one in range(size)] for offset in range(1, size)]


def place_of_source(place, offset, size):
    return place ^ offset if size & size - 1 == 0 else (place - offset) % size


def place_of_target(place, offset, size):
    return place ^ offset if size & size - 1 == 0 else (place + offset) % size


def shard_total(value, shards):
    if shards > 8:
        return lax.psum(value, "shard")
    tile = jnp.full((8, 128), value, jnp.float32)
    total = value
    for pairs in partners(shards):
        total = total + lax.ppermute(tile, "shard", pairs)[0, 0]
    return total


def rows_times_shards(full_rows, block, shards, place, encode, decode):
    if shards > 8:
        gathered = decode(lax.all_gather(encode(block), "shard", axis=0))
        return matmul(full_rows, gathered.reshape(-1, block.shape[1]))
    rows = block.shape[0]
    sent = encode(block)
    pieces = [block] + [decode(lax.ppermute(sent, "shard", pairs)) for pairs in partners(shards)]
    total = None
    for offset, piece in enumerate(pieces):
        source = place_of_source(place, offset, shards)
        left = lax.dynamic_slice_in_dim(full_rows, source * rows, rows, 1)
        term = matmul(left, piece)
        total = term if total is None else total + term
    return total


def scatter_product(full_rows, block, shards, place, encode, decode):
    if shards > 8:
        return lax.psum_scatter(
            matmul(full_rows.T, block), "shard", scatter_dimension=0, tiled=True
        )
    rows = full_rows.shape[1] // shards
    arrived = []
    for offset, pairs in enumerate(partners(shards), 1):
        target = place_of_target(place, offset, shards)
        chunk = matmul(lax.dynamic_slice_in_dim(full_rows, target * rows, rows, 1).T, block)
        arrived.append(lax.ppermute(encode(chunk), "shard", pairs))
    total = matmul(lax.dynamic_slice_in_dim(full_rows, place * rows, rows, 1).T, block)
    for payload in arrived:
        total = total + decode(payload)
    return total


def outer_block(gradient, grad_rows, shards, group, place, member):
    rows, cols = gradient.shape
    if rows % cols == 0 and shards <= 8:
        own = lax.dynamic_slice_in_dim(grad_rows, member * cols % rows, cols, 0)
        other = jnp.zeros_like(own)
        for offset in range(1, shards):
            pairs = []
            for column in range(group):
                home = column * cols // rows
                pairs.append((home * group + column, (home + offset) % shards * group + column))
            other = other + lax.ppermute(own, EVERY, pairs)
        partner = jnp.where(place == member * cols // rows, own, other)
        return jnp.dot(grad_rows, partner.T, preferred_element_type=jnp.float32)
    partner = lax.all_gather(gradient, "shard", axis=0, tiled=True)
    product = jnp.dot(gradient, partner.T, preferred_element_type=jnp.float32)
    return lax.psum_scatter(product, GROUP, scatter_dimension=1, tiled=True)


def on_device(
    gradient,
    gain_grad,
    left_statistic,
    left_basis,
    first_moment,
    second_moment,
    norm_gains,
    gain_first,
    gain_second,
):
    group = lax.axis_size(GROUP)
    shards = lax.axis_size("shard")
    place = lax.axis_index("shard")
    member = lax.axis_index(GROUP)
    rows, cols = gradient.shape
    grad_float = gradient.astype(jnp.float32)
    grad_rows = row_panel(gradient)
    late_basis, grad_rows = lax.optimization_barrier((left_basis, grad_rows))
    basis_rows = row_panel(late_basis)
    grad_rows_float = grad_rows.astype(jnp.float32)
    squares_total = shard_total(
        jnp.sum(grad_rows_float * grad_rows_float) + jnp.sum(gain_grad * gain_grad), shards
    )
    clip_factor = jnp.minimum(1.0, D / jnp.sqrt(squares_total + 1e-06))
    outer_part = outer_block(gradient, grad_rows, shards, group, place, member)
    new_statistic = 0.95 * left_statistic + 0.05 / D * clip_factor * clip_factor * outer_part
    ready_statistic, basis_rows = lax.optimization_barrier((new_statistic, basis_rows))
    statistic_rows = row_panel(ready_statistic)
    power_product = rows_times_shards(statistic_rows, left_basis, shards, place, same, same)
    power_rows = row_panel(power_product)
    rotated = clip_factor * scatter_product(basis_rows, grad_float, shards, place, same, same)
    new_first = 0.9 * first_moment + 0.1 * rotated
    new_second = 0.95 * second_moment + 0.05 * rotated * rotated
    direction = new_first / (jnp.sqrt(new_second) + 1e-08)
    update = rows_times_shards(
        basis_rows,
        direction,
        shards,
        place,
        lambda x: x.astype(jnp.float16),
        lambda x: x.astype(jnp.float32),
    )
    update, power_rows = lax.optimization_barrier((update, power_rows))
    power_sum = shard_total(jnp.sum(power_rows * power_rows), shards)
    scale = 0.9 * jnp.sqrt(D / (power_sum + 1e-06))
    iterate = scale * power_product
    iterate_rows = scale * power_rows
    row_index = place * rows + lax.broadcasted_iota(jnp.int32, (rows, cols), 0)
    col_index = member * cols + lax.broadcasted_iota(jnp.int32, (rows, cols), 1)
    eye = (row_index == col_index).astype(jnp.float32)
    for sweep_index in range(NS_STEPS):
        if sweep_index:
            iterate_rows = row_panel(iterate)
            gram_block = scatter_product(iterate_rows, iterate, shards, place, pack, unpack)
        else:
            gram_block = (
                scale
                * scale
                * scatter_product(power_rows, power_product, shards, place, pack, unpack)
            )
        iterate = iterate - 0.5 * rows_times_shards(
            iterate_rows, gram_block - eye, shards, place, pack, unpack
        )
    gain_clipped = clip_factor * gain_grad
    new_gain_first = 0.9 * gain_first + 0.1 * gain_clipped
    new_gain_second = 0.95 * gain_second + 0.05 * gain_clipped * gain_clipped
    new_gains = norm_gains - 0.01 * new_gain_first / (jnp.sqrt(new_gain_second) + 1e-08)
    return (
        update,
        new_first,
        new_second,
        new_statistic,
        iterate,
        new_gains,
        new_gain_first,
        new_gain_second,
    )


def solution(mesh):
    matrix = P("shard", GROUP)
    vector = P(None, "shard")
    return jax.shard_map(
        on_device,
        mesh=mesh,
        in_specs=(matrix, vector, matrix, matrix, matrix, matrix, vector, vector, vector),
        out_specs=(matrix, matrix, matrix, matrix, matrix, vector, vector, vector),
        check_vma=False,
    )
```

profile of v0, /device:TPU:8, one launch (start us, length us, event | category | flops | bytes accessed | tf_op | source)
XLA Modules:
  0.0 734.5 jit_solution(14928106622082852291)
XLA Ops:
  7.9 36.0 %all-gather.7.cloned.1.call-done = bf16[640,2560]{0,1:T(8,128)(2,1)} async-done(((bf16[640,320]{0,1:T(8,128)(2,1)}), bf16[640,2560]{0,1:T(8,128)(2,1)}) %all-gather.7.cloned.1.call-update) | async-done | bytes 3276816 | tf_op jit(solution)/shard_map/all_gather | solution.py:20
  67.2 43.5 %collective-permute-done = f32[8,128]{1,0:T(8,128)S(1)} collective-permute-done((f32[8,128]{1,0:T(8,128)S(1)}, f32[8,128]{1,0:T(8,128)S(1)}, u32[]{:S(2)}, u32[]{:S(2)}) %collective-permute-start) | collective-permute-done | bytes 4128 | tf_op jit(solution)/shard_map/ppermute | solution.py:60
  137.0 40.8 %all-gather.11.cloned.1.call-done = f32[640,2560]{0,1:T(8,128)} async-done(((f32[640,320]{0,1:T(8,128)}), f32[640,2560]{0,1:T(8,128)}) %all-gather.11.cloned.1.call-update) | async-done | bytes 6553616 | tf_op jit(solution)/shard_map/all_gather | solution.py:20
  202.0 29.3 %collective-permute-done.6 = f32[640,320]{0,1:T(8,128)S(1)} collective-permute-done((f32[640,320]{0,1:T(8,128)S(1)}, f32[640,320]{0,1:T(8,128)S(1)}, u32[]{:S(2)}, u32[]{:S(2)}) %collective-permute-start.6) | collective-permute-done | bytes 819232 | tf_op jit(solution)/shard_map/ppermute | solution.py:90
  231.3 23.9 %collective-permute-done.7 = f32[640,320]{0,1:T(8,128)S(1)} collective-permute-done((f32[640,320]{0,1:T(8,128)S(1)}, f32[640,320]{0,1:T(8,128)S(1)}, u32[]{:S(2)}, u32[]{:S(2)}) %collective-permute-start.7) | collective-permute-done | bytes 819232 | tf_op jit(solution)/shard_map/ppermute | solution.py:90
  255.2 16.5 %collective-permute-done.8 = f32[640,320]{0,1:T(8,128)S(1)} collective-permute-done((f32[640,320]{0,1:T(8,128)S(1)}, f32[640,320]{0,1:T(8,128)S(1)}, u32[]{:S(2)}, u32[]{:S(2)}) %collective-permute-start.8) | collective-permute-done | bytes 819232 | tf_op jit(solution)/shard_map/ppermute | solution.py:90
  280.4 21.3 %collective-permute-done.10 = f16[640,320]{0,1:T(8,128)(2,1)S(1)} collective-permute-done((f16[640,320]{0,1:T(8,128)(2,1)S(1)}, f16[640,320]{0,1:T(8,128)(2,1)S(1)}, u32[]{:S(2)}, u32[]{:S(2)}) %collective-permute-start.10) | collective-permute-done | bytes 409632 | tf_op jit(solution)/shard_map/ppermute | solution.py:70
  303.0 7.1 collective-permute-done.11
  331.4 24.1 %collective-permute-done.15 = f32[8,128]{1,0:T(8,128)S(1)} collective-permute-done((f32[8,128]{1,0:T(8,128)S(1)}, f32[8,128]{1,0:T(8,128)S(1)}, u32[]{:S(2)}, u32[]{:S(2)}) %collective-permute-start.15) | collective-permute-done | bytes 4128 | tf_op jit(solution)/shard_map/ppermute | solution.py:60
  357.3 7.6 %collective-permute-done.16 = f32[8,128]{1,0:T(8,128)S(1)} collective-permute-done((f32[8,128]{1,0:T(8,128)S(1)}, f32[8,128]{1,0:T(8,128)S(1)}, u32[]{:S(2)}, u32[]{:S(2)}) %collective-permute-start.16) | collective-permute-done | bytes 4128 | tf_op jit(solution)/shard_map/ppermute | solution.py:60
  381.2 25.5 %collective-permute-done.22 = f16[656,320]{0,1:T(8,128)(2,1)S(1)} collective-permute-done((f16[656,320]{0,1:T(8,128)(2,1)S(1)}, f16[656,320]{0,1:T(8,128)(2,1)S(1)}, u32[]{:S(2)}, u32[]{:S(2)}) %collective-permute-start.22) | collective-permute-done | bytes 419872 | tf_op jit(solution)/shard_map/ppermute | solution.py:70
  408.2 10.3 %collective-permute-done.23 = f16[656,320]{0,1:T(8,128)(2,1)S(1)} collective-permute-done((f16[656,320]{0,1:T(8,128)(2,1)S(1)}, f16[656,320]{0,1:T(8,128)(2,1)S(1)}, u32[]{:S(2)}, u32[]{:S(2)}) %collective-permute-start.23) | collective-permute-done | bytes 419872 | tf_op jit(solution)/shard_map/ppermute | solution.py:70
  423.0 46.7 %all-gather.15.cloned.1.call-done = f32[640,2560]{0,1:T(8,128)} async-done(((f32[640,320]{0,1:T(8,128)}), f32[640,2560]{0,1:T(8,128)}) %all-gather.15.cloned.1.call-update) | async-done | bytes 6553616 | tf_op jit(solution)/shard_map/all_gather | solution.py:20
  482.2 9.0 %collective-permute-done.24 = f16[656,320]{0,1:T(8,128)(2,1)S(1)} collective-permute-done((f16[656,320]{0,1:T(8,128)(2,1)S(1)}, f16[656,320]{0,1:T(8,128)(2,1)S(1)}, u32[]{:S(2)}, u32[]{:S(2)}) %collective-permute-start.24) | collective-permute-done | bytes 419872 | tf_op jit(solution)/shard_map/ppermute | solution.py:90
  491.2 21.4 %collective-permute-done.25 = f16[656,320]{0,1:T(8,128)(2,1)S(1)} collective-permute-done((f16[656,320]{0,1:T(8,128)(2,1)S(1)}, f16[656,320]{0,1:T(8,128)(2,1)S(1)}, u32[]{:S(2)}, u32[]{:S(2)}) %collective-permute-start.25) | collective-permute-done | bytes 419872 | tf_op jit(solution)/shard_map/ppermute | solution.py:90
  513.0 10.2 %collective-permute-done.26 = f16[656,320]{0,1:T(8,128)(2,1)S(1)} collective-permute-done((f16[656,320]{0,1:T(8,128)(2,1)S(1)}, f16[656,320]{0,1:T(8,128)(2,1)S(1)}, u32[]{:S(2)}, u32[]{:S(2)}) %collective-permute-start.26) | collective-permute-done | bytes 419872 | tf_op jit(solution)/shard_map/ppermute | solution.py:90
  531.5 27.0 %collective-permute-done.28 = f16[656,320]{0,1:T(8,128)(2,1)S(1)} collective-permute-done((f16[656,320]{0,1:T(8,128)(2,1)S(1)}, f16[656,320]{0,1:T(8,128)(2,1)S(1)}, u32[]{:S(2)}, u32[]{:S(2)}) %collective-permute-start.28) | collective-permute-done | bytes 419872 | tf_op jit(solution)/shard_map/ppermute | solution.py:70
  558.6 11.4 %collective-permute-done.29 = f16[656,320]{0,1:T(8,128)(2,1)S(1)} collective-permute-done((f16[656,320]{0,1:T(8,128)(2,1)S(1)}, f16[656,320]{0,1:T(8,128)(2,1)S(1)}, u32[]{:S(2)}, u32[]{:S(2)}) %collective-permute-start.29) | collective-permute-done | bytes 419872 | tf_op jit(solution)/shard_map/ppermute | solution.py:70
  575.9 44.9 %all-gather.17.cloned.1.call-done = f32[640,2560]{0,1:T(8,128)} async-done(((f32[640,320]{0,1:T(8,128)}), f32[640,2560]{0,1:T(8,128)}) %all-gather.17.cloned.1.call-update) | async-done | bytes 6553616 | tf_op jit(solution)/shard_map/all_gather | solution.py:20
  633.4 9.0 %collective-permute-done.30 = f16[656,320]{0,1:T(8,128)(2,1)S(1)} collective-permute-done((f16[656,320]{0,1:T(8,128)(2,1)S(1)}, f16[656,320]{0,1:T(8,128)(2,1)S(1)}, u32[]{:S(2)}, u32[]{:S(2)}) %collective-permute-start.30) | collective-permute-done | bytes 419872 | tf_op jit(solution)/shard_map/ppermute | solution.py:90
  642.5 21.4 %collective-permute-done.31 = f16[656,320]{0,1:T(8,128)(2,1)S(1)} collective-permute-done((f16[656,320]{0,1:T(8,128)(2,1)S(1)}, f16[656,320]{0,1:T(8,128)(2,1)S(1)}, u32[]{:S(2)}, u32[]{:S(2)}) %collective-permute-start.31) | collective-permute-done | bytes 419872 | tf_op jit(solution)/shard_map/ppermute | solution.py:90
  664.3 10.2 %collective-permute-done.32 = f16[656,320]{0,1:T(8,128)(2,1)S(1)} collective-permute-done((f16[656,320]{0,1:T(8,128)(2,1)S(1)}, f16[656,320]{0,1:T(8,128)(2,1)S(1)}, u32[]{:S(2)}, u32[]{:S(2)}) %collective-permute-start.32) | collective-permute-done | bytes 419872 | tf_op jit(solution)/shard_map/ppermute | solution.py:90
  683.4 26.4 %collective-permute-done.34 = f16[656,320]{0,1:T(8,128)(2,1)S(1)} collective-permute-done((f16[656,320]{0,1:T(8,128)(2,1)S(1)}, f16[656,320]{0,1:T(8,128)(2,1)S(1)}, u32[]{:S(2)}, u32[]{:S(2)}) %collective-permute-start.34) | collective-permute-done | bytes 419872 | tf_op jit(solution)/shard_map/ppermute | solution.py:70
  709.9 11.4 %collective-permute-done.35 = f16[656,320]{0,1:T(8,128)(2,1)S(1)} collective-permute-done((f16[656,320]{0,1:T(8,128)(2,1)S(1)}, f16[656,320]{0,1:T(8,128)(2,1)S(1)}, u32[]{:S(2)}, u32[]{:S(2)}) %collective-permute-start.35) | collective-permute-done | bytes 419872 | tf_op jit(solution)/shard_map/ppermute | solution.py:70
  (251 shorter events, 178.2 us)
Async XLA Ops:
  7.9 124.7 %all-gather.9.cloned.1.call-start = ((), (), s32[]{:S(2)}) async-start(), calls=%async_computation.1 | async-start | bytes 7372800 | tf_op jit(solution)/shard_map/all_gather | solution.py:20
  44.0 133.9 %all-gather.11.cloned.1.call-start = ((), (), s32[]{:S(2)}) async-start(), calls=%async_computation.2 | async-start | bytes 7372800 | tf_op jit(solution)/shard_map/all_gather | solution.py:20
  52.2 63.3 %collective-permute-start.3 = (bf16[320,2560]{1,0:T(8,128)(2,1)}, bf16[320,2560]{1,0:T(8,128)(2,1)}, u32[]{:S(2)}, u32[]{:S(2)}) collective-permute-start(bf16[320,2560]{1,0:T(8,128)(2,1)} %copy.18), channel_id=1, source_target_pairs={{0,8},{1,9},{10,18},{11,19},{20,28},{21,29},{30,6},{31,7}} | collective-permute-start | bytes 4915208 | tf_op jit(solution)/shard_map/ppermute | solution.py:107
  53.5 65.9 %collective-permute-start.4 = (bf16[320,2560]{1,0:T(8,128)(2,1)}, bf16[320,2560]{1,0:T(8,128)(2,1)}, u32[]{:S(2)}, u32[]{:S(2)}) collective-permute-start(bf16[320,2560]{1,0:T(8,128)(2,1)} %copy.18), channel_id=1, source_target_pairs={{0,16},{1,17},{10,26},{11,27},{20,4},{21,5},{30,14},{31,15}} | collective-permute-start | bytes 4915208 | tf_op jit(solution)/shard_map/ppermute | solution.py:107
  55.4 67.9 %collective-permute-start.5 = (bf16[320,2560]{1,0:T(8,128)(2,1)}, bf16[320,2560]{1,0:T(8,128)(2,1)}, u32[]{:S(2)}, u32[]{:S(2)}) collective-permute-start(bf16[320,2560]{1,0:T(8,128)(2,1)} %copy.18), channel_id=1, source_target_pairs={{0,24},{1,25},{10,2},{11,3},{20,12},{21,13},{30,22},{31,23}} | collective-permute-start | bytes 4915208 | tf_op jit(solution)/shard_map/ppermute | solution.py:107
  61.4 49.3 %collective-permute-start = (f32[8,128]{1,0:T(8,128)S(1)}, f32[8,128]{1,0:T(8,128)S(1)}, u32[]{:S(2)}, u32[]{:S(2)}) collective-permute-start(f32[8,128]{1,0:T(8,128)S(1)} %broadcast_in_dim.28), channel_id=1, source_target_pairs={{0,8},{8,0},{16,24},{24,16},{1,9},{9,1},{17,25},{25,17},{2,10},{10... | collective-permute-start | bytes 12296 | tf_op jit(solution)/shard_map/ppermute | solution.py:60
  67.2 44.7 %collective-permute-start.1 = (f32[8,128]{1,0:T(8,128)S(1)}, f32[8,128]{1,0:T(8,128)S(1)}, u32[]{:S(2)}, u32[]{:S(2)}) collective-permute-start(f32[8,128]{1,0:T(8,128)S(1)} %broadcast_in_dim.28), channel_id=1, source_target_pairs={{0,16},{8,24},{16,0},{24,8},{1,17},{9,25},{17,1},{25,9},{2,18},{10... | collective-permute-start | bytes 12296 | tf_op jit(solution)/shard_map/ppermute | solution.py:60
  132.6 181.2 %all-gather.13.cloned.1.call-start = ((), (), s32[]{:S(2)}) async-start(), calls=%async_computation.3 | async-start | bytes 7372800 | tf_op jit(solution)/shard_map/all_gather | solution.py:20
  132.6 48.3 %collective-permute-start.14 = (f32[640,320]{0,1:T(8,128)}, f32[640,320]{0,1:T(8,128)S(1)}, u32[]{:S(2)}, u32[]{:S(2)}) collective-permute-start(f32[640,320]{0,1:T(8,128)} %param.12), channel_id=1, source_target_pairs={{0,24},{8,16},{16,8},{24,0},{1,25},{9,17},{17,9},{25,1},{2,26},{10... | collective-permute-start | bytes 2457608 | tf_op jit(solution)/shard_map/ppermute | solution.py:70
  133.5 53.0 %collective-permute-start.13 = (f32[640,320]{0,1:T(8,128)}, f32[640,320]{0,1:T(8,128)S(1)}, u32[]{:S(2)}, u32[]{:S(2)}) collective-permute-start(f32[640,320]{0,1:T(8,128)} %param.12), channel_id=1, source_target_pairs={{0,16},{8,24},{16,0},{24,8},{1,17},{9,25},{17,1},{25,9},{2,18},{10... | collective-permute-start | bytes 2457608 | tf_op jit(solution)/shard_map/ppermute | solution.py:70
  137.0 50.8 %collective-permute-start.12 = (f32[640,320]{0,1:T(8,128)}, f32[640,320]{0,1:T(8,128)S(1)}, u32[]{:S(2)}, u32[]{:S(2)}) collective-permute-start(f32[640,320]{0,1:T(8,128)} %param.12), channel_id=1, source_target_pairs={{0,8},{8,0},{16,24},{24,16},{1,9},{9,1},{17,25},{25,17},{2,10},{10... | collective-permute-start | bytes 2457608 | tf_op jit(solution)/shard_map/ppermute | solution.py:70
  190.1 279.5 %all-gather.15.cloned.1.call-start = ((), (), s32[]{:S(2)}) async-start(), calls=%async_computation.4 | async-start | bytes 7372800 | tf_op jit(solution)/shard_map/all_gather | solution.py:20
  200.4 54.8 %collective-permute-start.7 = (f32[640,320]{0,1:T(8,128)S(1)}, f32[640,320]{0,1:T(8,128)S(1)}, u32[]{:S(2)}, u32[]{:S(2)}) collective-permute-start(f32[640,320]{0,1:T(8,128)S(1)} %fusion.67), channel_id=1, source_target_pairs={{0,16},{8,24},{16,0},{24,8},{1,17},{9,25},{17,1},{25,9},{2,18},{10... | collective-permute-start | bytes 2457608 | tf_op jit(solution)/shard_map/ppermute | solution.py:90
  201.4 70.3 %collective-permute-start.8 = (f32[640,320]{0,1:T(8,128)S(1)}, f32[640,320]{0,1:T(8,128)S(1)}, u32[]{:S(2)}, u32[]{:S(2)}) collective-permute-start(f32[640,320]{0,1:T(8,128)S(1)} %fusion.63), channel_id=1, source_target_pairs={{0,24},{8,16},{16,8},{24,0},{1,25},{9,17},{17,9},{25,1},{2,26},{10... | collective-permute-start | bytes 2457608 | tf_op jit(solution)/shard_map/ppermute | solution.py:90
  322.0 47.1 %collective-permute-start.18 = (f16[656,320]{0,1:T(8,128)(2,1)S(1)}, f16[656,320]{0,1:T(8,128)(2,1)S(1)}, u32[]{:S(2)}, u32[]{:S(2)}) collective-permute-start(f16[656,320]{0,1:T(8,128)(2,1)S(1)} %pad_maximum_fusion), channel_id=1, source_target_pairs={{0,8},{8,0},{16,24},{24,16},{1,9},{9,1},{17,25},{25,17},{2,10},{10... | collective-permute-start | bytes 1259528 | tf_op jit(solution)/shard_map/ppermute | solution.py:90
  322.5 46.7 %collective-permute-start.19 = (f16[656,320]{0,1:T(8,128)(2,1)S(1)}, f16[656,320]{0,1:T(8,128)(2,1)S(1)}, u32[]{:S(2)}, u32[]{:S(2)}) collective-permute-start(f16[656,320]{0,1:T(8,128)(2,1)S(1)} %pad_maximum_fusion.1), channel_id=1, source_target_pairs={{0,16},{8,24},{16,0},{24,8},{1,17},{9,25},{17,1},{25,9},{2,18},{10... | collective-permute-start | bytes 1259528 | tf_op jit(solution)/shard_map/ppermute | solution.py:90
  324.8 44.8 %collective-permute-start.20 = (f16[656,320]{0,1:T(8,128)(2,1)S(1)}, f16[656,320]{0,1:T(8,128)(2,1)}, u32[]{:S(2)}, u32[]{:S(2)}) collective-permute-start(f16[656,320]{0,1:T(8,128)(2,1)S(1)} %pad_maximum_fusion.2), channel_id=1, source_target_pairs={{0,24},{8,16},{16,8},{24,0},{1,25},{9,17},{17,9},{25,1},{2,26},{10... | collective-permute-start | bytes 1259528 | tf_op jit(solution)/shard_map/ppermute | solution.py:90
  376.9 41.6 %collective-permute-start.23 = (f16[656,320]{0,1:T(8,128)(2,1)S(1)}, f16[656,320]{0,1:T(8,128)(2,1)S(1)}, u32[]{:S(2)}, u32[]{:S(2)}) collective-permute-start(f16[656,320]{0,1:T(8,128)(2,1)S(1)} %pad_maximum_fusion.3), channel_id=1, source_target_pairs={{0,24},{8,16},{16,8},{24,0},{1,25},{9,17},{17,9},{25,1},{2,26},{10... | collective-permute-start | bytes 1259528 | tf_op jit(solution)/shard_map/ppermute | solution.py:70
  422.9 198.0 %all-gather.17.cloned.1.call-start = ((), (), s32[]{:S(2)}) async-start(), calls=%async_computation.5 | async-start | bytes 7372800 | tf_op jit(solution)/shard_map/all_gather | solution.py:20
  525.8 44.2 %collective-permute-start.29 = (f16[656,320]{0,1:T(8,128)(2,1)S(1)}, f16[656,320]{0,1:T(8,128)(2,1)S(1)}, u32[]{:S(2)}, u32[]{:S(2)}) collective-permute-start(f16[656,320]{0,1:T(8,128)(2,1)S(1)} %pad_maximum_fusion.7), channel_id=1, source_target_pairs={{0,24},{8,16},{16,8},{24,0},{1,25},{9,17},{17,9},{25,1},{2,26},{10... | collective-permute-start | bytes 1259528 | tf_op jit(solution)/shard_map/ppermute | solution.py:70
  527.6 42.8 %collective-permute-start.27 = (f16[656,320]{0,1:T(8,128)(2,1)S(1)}, f16[656,320]{0,1:T(8,128)(2,1)S(1)}, u32[]{:S(2)}, u32[]{:S(2)}) collective-permute-start(f16[656,320]{0,1:T(8,128)(2,1)S(1)} %pad_maximum_fusion.7), channel_id=1, source_target_pairs={{0,8},{8,0},{16,24},{24,16},{1,9},{9,1},{17,25},{25,17},{2,10},{10... | collective-permute-start | bytes 1259528 | tf_op jit(solution)/shard_map/ppermute | solution.py:70
  633.1 41.4 %collective-permute-start.32 = (f16[656,320]{0,1:T(8,128)(2,1)S(1)}, f16[656,320]{0,1:T(8,128)(2,1)S(1)}, u32[]{:S(2)}, u32[]{:S(2)}) collective-permute-start(f16[656,320]{0,1:T(8,128)(2,1)S(1)} %pad_maximum_fusion.10), channel_id=1, source_target_pairs={{0,24},{8,16},{16,8},{24,0},{1,25},{9,17},{17,9},{25,1},{2,26},{10... | collective-permute-start | bytes 1259528 | tf_op jit(solution)/shard_map/ppermute | solution.py:90
  677.1 44.2 %collective-permute-start.35 = (f16[656,320]{0,1:T(8,128)(2,1)S(1)}, f16[656,320]{0,1:T(8,128)(2,1)S(1)}, u32[]{:S(2)}, u32[]{:S(2)}) collective-permute-start(f16[656,320]{0,1:T(8,128)(2,1)S(1)} %pad_maximum_fusion.11), channel_id=1, source_target_pairs={{0,24},{8,16},{16,8},{24,0},{1,25},{9,17},{17,9},{25,1},{2,26},{10... | collective-permute-start | bytes 1259528 | tf_op jit(solution)/shard_map/ppermute | solution.py:70
  679.5 42.2 %collective-permute-start.33 = (f16[656,320]{0,1:T(8,128)(2,1)S(1)}, f16[656,320]{0,1:T(8,128)(2,1)S(1)}, u32[]{:S(2)}, u32[]{:S(2)}) collective-permute-start(f16[656,320]{0,1:T(8,128)(2,1)S(1)} %pad_maximum_fusion.11), channel_id=1, source_target_pairs={{0,8},{8,0},{16,24},{24,16},{1,9},{9,1},{17,25},{25,17},{2,10},{10... | collective-permute-start | bytes 1259528 | tf_op jit(solution)/shard_map/ppermute | solution.py:70
  (39 other events, 941.7 us)
Sparse Core Ops, SparseCore 0:
  9.9 34.0 all-gather.6
  45.8 46.6 all-gather.8
  132.7 45.0 all-gather.10
  190.2 47.2 all-gather.12
  423.0 46.5 all-gather.14
  576.1 44.7 all-gather.16
where the time goes:
time: 743 us; the launch traced here: 734 us
  waiting for transfers between devices  542 us (73%)
  matrix products  81.2 us (11%)
  starting transfers between devices  49.9 us (7%)
  local copies, waits for them, and re-layouts  25 us (3%)
  between operations  21.4 us (3%)
  other arithmetic  15.3 us (2%)
    all_gather x6, waiting for transfers between devices, row_panel(): return lax.all_gather(local_block, GROUP, axis=1, tiled=True)  168 us
    ppermute x12, waiting for transfers between devices, scatter_product(): arrived.append(lax.ppermute(encode(chunk), 'shard', pairs))  151 us
    ppermute x15, waiting for transfers between devices, rows_times_shards(): lax.ppermute(sent, 'shard', pairs)  143 us
    ppermute x6, waiting for transfers between devices, shard_total(): total = total + lax.ppermute(tile, 'shard', pairs)[0, 0]  78.2 us
    dot_general x36, matrix products, matmul(): jnp.dot(left_side, right_side, precision=lax.Precision.HIGH, preferred_el...  75.7 us
    ppermute x15, starting transfers between devices, rows_times_shards(): lax.ppermute(sent, 'shard', pairs)  22.2 us
  transfers between devices with their start and end apart: 42, of which 27 were waited for; matrix products, arithmetic and copies ran while one was open for 11% of the time, Pallas kernels for 0%

commit v1 on v0

--- a/solution.py
+++ b/solution.py
@@ -10,6 +10,27 @@
 PAD = 16
 
 
+def ring_gather(x, axis, dim):
+    count, index, rows = (lax.axis_size(axis), lax.axis_index(axis), x.shape[dim])
+    ahead = [(i, (i + 1) % count) for i in range(count)]
+    left = [(i, (i - 1) % count) for i in range(count)]
+    out = jnp.zeros((*x.shape[:dim], count * rows, *x.shape[dim + 1 :]), x.dtype)
+    out = lax.dynamic_update_slice_in_dim(out, x, index * rows, axis=dim)
+    from_left = from_right = x
+    middle = count // 2
+    for step in range(1, middle + 1):
+        from_left = lax.ppermute(from_left, axis, ahead)
+        out = lax.dynamic_update_slice_in_dim(
+            out, from_left, (index - step) % count * rows, axis=dim
+        )
+        if step < count - middle:
+            from_right = lax.ppermute(from_right, axis, left)
+            out = lax.dynamic_update_slice_in_dim(
+                out, from_right, (index + step) % count * rows, axis=dim
+            )
+    return out
+
+
 def matmul(left_side, right_side):
     return jnp.dot(
         left_side, right_side, precision=lax.Precision.HIGH, preferred_element_type=jnp.float32
@@ -17,7 +38,7 @@
 
 
 def row_panel(local_block):
-    return lax.all_gather(local_block, GROUP, axis=1, tiled=True)
+    return ring_gather(local_block, GROUP, 1)
 
 
 def same(block):

time: 743 us -> 1110 us (1.49)
  waiting for transfers between devices: 542 us -> 814 us
  local copies, waits for them, and re-layouts: 25 us -> 88.5 us
  starting transfers between devices: 49.9 us -> 96.5 us
  between operations: 21.4 us -> 8.29 us
    ppermute x0 -> x42, waiting for transfers between devices: none -> 505 us  [the longest x24 315 us: ring_gather(): from_left = lax.ppermute(from_left, axis, ahead)]
    all_gather x6 -> x0, waiting for transfers between devices: 168 us -> none  [row_panel(): return lax.all_gather(local_block, GROUP, axis=1, tiled=True)]
    dynamic_update_slice x0 -> x45, local copies, waits for them, and re-layouts: none -> 73.8 us  [the longest x24 36.9 us: ring_gather(): lax.dynamic_update_slice_in_dim(out, from_left, (index - step) % count *...]
    ppermute x0 -> x42, starting transfers between devices: none -> 53 us  [the longest x18 27.7 us: ring_gather(): from_right = lax.ppermute(from_right, axis, left)]
    ppermute x6, waiting for transfers between devices: 78.2 us -> 35.3 us  [shard_total(): total = total + lax.ppermute(tile, 'shard', pairs)[0, 0]]
    ppermute x12, waiting for transfers between devices: 151 us -> 136 us  [scatter_product(): arrived.append(lax.ppermute(encode(chunk), 'shard', pairs))]
    ppermute x3 -> x0, local copies, waits for them, and re-layouts: 11.6 us -> none  [outer_block(): other = other + lax.ppermute(own, EVERY, pairs)]
  transfers between devices with their start and end apart: 42 -> 78, of which waited for: 27 -> 59; matrix products, arithmetic and copies ran while one was open for 11% -> 12% of each run, Pallas kernels for 0% -> 0%
where the time goes in v1:
time: 1110 us; the launch traced here: 1100 us
  waiting for transfers between devices  814 us (73%)
  starting transfers between devices  96.5 us (9%)
  local copies, waits for them, and re-layouts  88.5 us (8%)
  matrix products  72.4 us (7%)
  other arithmetic  19.1 us (2%)
    ppermute x24, waiting for transfers between devices, ring_gather(): from_left = lax.ppermute(from_left, axis, ahead)  315 us
    ppermute x18, waiting for transfers between devices, ring_gather(): from_right = lax.ppermute(from_right, axis, left)  190 us
    ppermute x15, waiting for transfers between devices, rows_times_shards(): lax.ppermute(sent, 'shard', pairs)  138 us
    ppermute x12, waiting for transfers between devices, scatter_product(): arrived.append(lax.ppermute(encode(chunk), 'shard', pairs))  136 us
    dot_general x36, matrix products, matmul(): jnp.dot(left_side, right_side, precision=lax.Precision.HIGH, preferred_el...  68.4 us
    dynamic_update_slice x24, local copies, waits for them, and re-layouts, ring_gather(): lax.dynamic_update_slice_in_dim(out, from_left, (index - step) % count *...  36.9 us
    ppermute x6, waiting for transfers between devices, shard_total(): total = total + lax.ppermute(tile, 'shard', pairs)[0, 0]  35.3 us
    dynamic_update_slice x18, local copies, waits for them, and re-layouts, ring_gather(): lax.dynamic_update_slice_in_dim(out, from_right, (index + step) % count *...  28.5 us
  transfers between devices with their start and end apart: 78, of which 59 were waited for; matrix products, arithmetic and copies ran while one was open for 12% of the time, Pallas kernels for 0%

profile of v1, /device:TPU:8, one launch (start us, length us, event | category | flops | bytes accessed | tf_op | source)
XLA Modules:
  0.0 1098.6 jit_solution(13016432669606429519)
XLA Ops:
  155.4 15.1 %collective-permute-done.15 = f32[640,320]{0,1:T(8,128)} collective-permute-done((f32[640,320]{0,1:T(8,128)}, f32[640,320]{0,1:T(8,128)}, u32[]{:S(2)}, u32[]{:S(2)}) %collective-permute-start.15) | collective-permute-done | bytes 819232 | tf_op jit(solution)/shard_map/ppermute | solution.py:22
  243.3 18.7 %collective-permute-done.26 = f32[640,320]{0,1:T(8,128)S(1)} collective-permute-done((f32[640,320]{0,1:T(8,128)S(1)}, f32[640,320]{0,1:T(8,128)S(1)}, u32[]{:S(2)}, u32[]{:S(2)}) %collective-permute-start.26) | collective-permute-done | bytes 819232 | tf_op jit(solution)/shard_map/ppermute | solution.py:22
  262.0 16.6 %collective-permute-done.27 = f32[640,320]{0,1:T(8,128)} collective-permute-done((f32[640,320]{0,1:T(8,128)S(1)}, f32[640,320]{0,1:T(8,128)}, u32[]{:S(2)}, u32[]{:S(2)}) %collective-permute-start.27) | collective-permute-done | bytes 819232 | tf_op jit(solution)/shard_map/ppermute | solution.py:27
  279.8 17.4 %collective-permute-done.28 = f32[640,320]{0,1:T(8,128)} collective-permute-done((f32[640,320]{0,1:T(8,128)S(1)}, f32[640,320]{0,1:T(8,128)}, u32[]{:S(2)}, u32[]{:S(2)}) %collective-permute-start.28) | collective-permute-done | bytes 819232 | tf_op jit(solution)/shard_map/ppermute | solution.py:22
  348.8 18.0 %collective-permute-done.32 = f32[640,320]{0,1:T(8,128)S(1)} collective-permute-done((f32[640,320]{0,1:T(8,128)}, f32[640,320]{0,1:T(8,128)S(1)}, u32[]{:S(2)}, u32[]{:S(2)}) %collective-permute-start.32) | collective-permute-done | bytes 819232 | tf_op jit(solution)/shard_map/ppermute | solution.py:22
  396.4 15.2 %collective-permute-done.20 = f32[640,320]{0,1:T(8,128)S(1)} collective-permute-done((f32[640,320]{0,1:T(8,128)S(1)}, f32[640,320]{0,1:T(8,128)S(1)}, u32[]{:S(2)}, u32[]{:S(2)}) %collective-permute-start.20) | collective-permute-done | bytes 819232 | tf_op jit(solution)/shard_map/ppermute | solution.py:111
  411.6 22.7 %collective-permute-done.21 = f32[640,320]{0,1:T(8,128)S(1)} collective-permute-done((f32[640,320]{0,1:T(8,128)S(1)}, f32[640,320]{0,1:T(8,128)S(1)}, u32[]{:S(2)}, u32[]{:S(2)}) %collective-permute-start.21) | collective-permute-done | bytes 819232 | tf_op jit(solution)/shard_map/ppermute | solution.py:111
  434.3 16.7 %collective-permute-done.22 = f32[640,320]{0,1:T(8,128)S(1)} collective-permute-done((f32[640,320]{0,1:T(8,128)S(1)}, f32[640,320]{0,1:T(8,128)S(1)}, u32[]{:S(2)}, u32[]{:S(2)}) %collective-permute-start.22) | collective-permute-done | bytes 819232 | tf_op jit(solution)/shard_map/ppermute | solution.py:111
  515.2 16.7 %collective-permute-done.42 = f32[640,320]{0,1:T(8,128)S(1)} collective-permute-done((f32[640,320]{0,1:T(8,128)S(1)}, f32[640,320]{0,1:T(8,128)S(1)}, u32[]{:S(2)}, u32[]{:S(2)}) %collective-permute-start.42) | collective-permute-done | bytes 819232 | tf_op jit(solution)/shard_map/ppermute | solution.py:22
  548.1 24.6 %collective-permute-done.43 = f32[8,128]{1,0:T(8,128)S(1)} collective-permute-done((f32[8,128]{1,0:T(8,128)S(1)}, f32[8,128]{1,0:T(8,128)S(1)}, u32[]{:S(2)}, u32[]{:S(2)}) %collective-permute-start.43) | collective-permute-done | bytes 4128 | tf_op jit(solution)/shard_map/ppermute | solution.py:81
  601.9 25.8 %collective-permute-done.50 = f16[656,320]{0,1:T(8,128)(2,1)S(1)} collective-permute-done((f16[656,320]{0,1:T(8,128)(2,1)S(1)}, f16[656,320]{0,1:T(8,128)(2,1)S(1)}, u32[]{:S(2)}, u32[]{:S(2)}) %collective-permute-start.50) | collective-permute-done | bytes 419872 | tf_op jit(solution)/shard_map/ppermute | solution.py:91
  647.5 18.6 %collective-permute-done.52 = f32[640,320]{0,1:T(8,128)S(1)} collective-permute-done((f32[640,320]{0,1:T(8,128)S(1)}, f32[640,320]{0,1:T(8,128)S(1)}, u32[]{:S(2)}, u32[]{:S(2)}) %collective-permute-start.52) | collective-permute-done | bytes 819232 | tf_op jit(solution)/shard_map/ppermute | solution.py:22
  668.5 15.5 %collective-permute-done.53 = f32[640,320]{0,1:T(8,128)S(1)} collective-permute-done((f32[640,320]{0,1:T(8,128)S(1)}, f32[640,320]{0,1:T(8,128)S(1)}, u32[]{:S(2)}, u32[]{:S(2)}) %collective-permute-start.53) | collective-permute-done | bytes 819232 | tf_op jit(solution)/shard_map/ppermute | solution.py:27
  703.7 15.5 %collective-permute-done.55 = f32[640,320]{0,1:T(8,128)S(1)} collective-permute-done((f32[640,320]{0,1:T(8,128)S(1)}, f32[640,320]{0,1:T(8,128)S(1)}, u32[]{:S(2)}, u32[]{:S(2)}) %collective-permute-start.55) | collective-permute-done | bytes 819232 | tf_op jit(solution)/shard_map/ppermute | solution.py:27
  754.3 17.1 %collective-permute-done.58 = f32[640,320]{0,1:T(8,128)S(1)} collective-permute-done((f32[640,320]{0,1:T(8,128)S(1)}, f32[640,320]{0,1:T(8,128)S(1)}, u32[]{:S(2)}, u32[]{:S(2)}) %collective-permute-start.58) | collective-permute-done | bytes 819232 | tf_op jit(solution)/shard_map/ppermute | solution.py:22
  876.9 18.9 %collective-permute-done.65 = f32[640,320]{0,1:T(8,128)S(1)} collective-permute-done((f32[640,320]{0,1:T(8,128)S(1)}, f32[640,320]{0,1:T(8,128)S(1)}, u32[]{:S(2)}, u32[]{:S(2)}) %collective-permute-start.65) | collective-permute-done | bytes 819232 | tf_op jit(solution)/shard_map/ppermute | solution.py:22
  895.8 16.6 %collective-permute-done.66 = f32[640,320]{0,1:T(8,128)S(1)} collective-permute-done((f32[640,320]{0,1:T(8,128)S(1)}, f32[640,320]{0,1:T(8,128)S(1)}, u32[]{:S(2)}, u32[]{:S(2)}) %collective-permute-start.66) | collective-permute-done | bytes 819232 | tf_op jit(solution)/shard_map/ppermute | solution.py:27
  913.3 17.5 %collective-permute-done.67 = f32[640,320]{0,1:T(8,128)S(1)} collective-permute-done((f32[640,320]{0,1:T(8,128)S(1)}, f32[640,320]{0,1:T(8,128)S(1)}, u32[]{:S(2)}, u32[]{:S(2)}) %collective-permute-start.67) | collective-permute-done | bytes 819232 | tf_op jit(solution)/shard_map/ppermute | solution.py:22
  930.9 16.6 %collective-permute-done.68 = f32[640,320]{0,1:T(8,128)S(1)} collective-permute-done((f32[640,320]{0,1:T(8,128)S(1)}, f32[640,320]{0,1:T(8,128)S(1)}, u32[]{:S(2)}, u32[]{:S(2)}) %collective-permute-start.68) | collective-permute-done | bytes 819232 | tf_op jit(solution)/shard_map/ppermute | solution.py:27
  948.5 17.5 %collective-permute-done.69 = f32[640,320]{0,1:T(8,128)S(1)} collective-permute-done((f32[640,320]{0,1:T(8,128)S(1)}, f32[640,320]{0,1:T(8,128)S(1)}, u32[]{:S(2)}, u32[]{:S(2)}) %collective-permute-start.69) | collective-permute-done | bytes 819232 | tf_op jit(solution)/shard_map/ppermute | solution.py:22
  966.3 16.2 %collective-permute-done.70 = f32[640,320]{0,1:T(8,128)S(1)} collective-permute-done((f32[640,320]{0,1:T(8,128)S(1)}, f32[640,320]{0,1:T(8,128)S(1)}, u32[]{:S(2)}, u32[]{:S(2)}) %collective-permute-start.70) | collective-permute-done | bytes 819232 | tf_op jit(solution)/shard_map/ppermute | solution.py:27
  982.6 16.4 %collective-permute-done.71 = f32[640,320]{0,1:T(8,128)S(1)} collective-permute-done((f32[640,320]{0,1:T(8,128)S(1)}, f32[640,320]{0,1:T(8,128)S(1)}, u32[]{:S(2)}, u32[]{:S(2)}) %collective-permute-start.71) | collective-permute-done | bytes 819232 | tf_op jit(solution)/shard_map/ppermute | solution.py:22
  1020.9 17.6 %collective-permute-done.73 = f16[656,320]{0,1:T(8,128)(2,1)S(1)} collective-permute-done((f16[656,320]{0,1:T(8,128)(2,1)S(1)}, f16[656,320]{0,1:T(8,128)(2,1)S(1)}, u32[]{:S(2)}, u32[]{:S(2)}) %collective-permute-start.73) | collective-permute-done | bytes 419872 | tf_op jit(solution)/shard_map/ppermute | solution.py:111
  1068.2 16.9 %collective-permute-done.76 = f16[656,320]{0,1:T(8,128)(2,1)S(1)} collective-permute-done((f16[656,320]{0,1:T(8,128)(2,1)S(1)}, f16[656,320]{0,1:T(8,128)(2,1)S(1)}, u32[]{:S(2)}, u32[]{:S(2)}) %collective-permute-start.76) | collective-permute-done | bytes 419872 | tf_op jit(solution)/shard_map/ppermute | solution.py:91
  (360 shorter events, 661.8 us)
Async XLA Ops:
  49.6 50.7 %collective-permute-start.5 = (bf16[640,320]{1,0:T(8,128)(2,1)}, bf16[640,320]{1,0:T(8,128)(2,1)}, u32[]{:S(2)}, u32[]{:S(2)}) collective-permute-start(bf16[640,320]{1,0:T(8,128)(2,1)} %collective-permute-done.3), channel_id=1, source_target_pairs={{0,7},{1,0},{2,1},{3,2},{4,3},{5,4},{6,5},{7,6},{8,15},{9,8},{10,9... | collective-permute-start | bytes 1228808 | tf_op jit(solution)/shard_map/ppermute | solution.py:27
  59.4 48.0 %collective-permute-start.6 = (bf16[640,320]{1,0:T(8,128)(2,1)}, bf16[640,320]{1,0:T(8,128)(2,1)}, u32[]{:S(2)}, u32[]{:S(2)}) collective-permute-start(bf16[640,320]{1,0:T(8,128)(2,1)} %collective-permute-done.4), channel_id=1, source_target_pairs={{0,1},{1,2},{2,3},{3,4},{4,5},{5,6},{6,7},{7,0},{8,9},{9,10},{10,1... | collective-permute-start | bytes 1228808 | tf_op jit(solution)/shard_map/ppermute | solution.py:22
  137.6 70.2 %collective-permute-start.10 = (bf16[320,2560]{1,0:T(8,128)(2,1)}, bf16[320,2560]{1,0:T(8,128)(2,1)}, u32[]{:S(2)}, u32[]{:S(2)}) collective-permute-start(bf16[320,2560]{1,0:T(8,128)(2,1)} %constant_dynamic-slice_fusion), channel_id=1, source_target_pairs={{0,8},{1,9},{10,18},{11,19},{20,28},{21,29},{30,6},{31,7}} | collective-permute-start | bytes 4915208 | tf_op jit(solution)/shard_map/ppermute | solution.py:128
  138.9 68.9 %collective-permute-start.11 = (bf16[320,2560]{1,0:T(8,128)(2,1)}, bf16[320,2560]{1,0:T(8,128)(2,1)}, u32[]{:S(2)}, u32[]{:S(2)}) collective-permute-start(bf16[320,2560]{1,0:T(8,128)(2,1)} %constant_dynamic-slice_fusion), channel_id=1, source_target_pairs={{0,16},{1,17},{10,26},{11,27},{20,4},{21,5},{30,14},{31,15}} | collective-permute-start | bytes 4915208 | tf_op jit(solution)/shard_map/ppermute | solution.py:128
  140.8 67.0 %collective-permute-start.12 = (bf16[320,2560]{1,0:T(8,128)(2,1)}, bf16[320,2560]{1,0:T(8,128)(2,1)}, u32[]{:S(2)}, u32[]{:S(2)}) collective-permute-start(bf16[320,2560]{1,0:T(8,128)(2,1)} %constant_dynamic-slice_fusion), channel_id=1, source_target_pairs={{0,24},{1,25},{10,2},{11,3},{20,12},{21,13},{30,22},{31,23}} | collective-permute-start | bytes 4915208 | tf_op jit(solution)/shard_map/ppermute | solution.py:128
  240.6 38.0 %collective-permute-start.27 = (f32[640,320]{0,1:T(8,128)S(1)}, f32[640,320]{0,1:T(8,128)}, u32[]{:S(2)}, u32[]{:S(2)}) collective-permute-start(f32[640,320]{0,1:T(8,128)S(1)} %fusion.188), channel_id=1, source_target_pairs={{0,7},{1,0},{2,1},{3,2},{4,3},{5,4},{6,5},{7,6},{8,15},{9,8},{10,9... | collective-permute-start | bytes 2457608 | tf_op jit(solution)/shard_map/ppermute | solution.py:27
  297.4 69.4 %collective-permute-start.34 = (f32[640,320]{0,1:T(8,128)}, f32[640,320]{0,1:T(8,128)S(1)}, u32[]{:S(2)}, u32[]{:S(2)}) collective-permute-start(f32[640,320]{0,1:T(8,128)} %param.12), channel_id=1, source_target_pairs={{0,16},{8,24},{16,0},{24,8},{1,17},{9,25},{17,1},{25,9},{2,18},{10... | collective-permute-start | bytes 2457608 | tf_op jit(solution)/shard_map/ppermute | solution.py:91
  300.0 68.1 %collective-permute-start.33 = (f32[640,320]{0,1:T(8,128)}, f32[640,320]{0,1:T(8,128)}, u32[]{:S(2)}, u32[]{:S(2)}) collective-permute-start(f32[640,320]{0,1:T(8,128)} %param.12), channel_id=1, source_target_pairs={{0,8},{8,0},{16,24},{24,16},{1,9},{9,1},{17,25},{25,17},{2,10},{10... | collective-permute-start | bytes 2457608 | tf_op jit(solution)/shard_map/ppermute | solution.py:91
  300.5 70.1 %collective-permute-start.35 = (f32[640,320]{0,1:T(8,128)}, f32[640,320]{0,1:T(8,128)S(1)}, u32[]{:S(2)}, u32[]{:S(2)}) collective-permute-start(f32[640,320]{0,1:T(8,128)} %param.12), channel_id=1, source_target_pairs={{0,24},{8,16},{16,8},{24,0},{1,25},{9,17},{17,9},{25,1},{2,26},{10... | collective-permute-start | bytes 2457608 | tf_op jit(solution)/shard_map/ppermute | solution.py:91
  377.6 56.6 %collective-permute-start.21 = (f32[640,320]{0,1:T(8,128)S(1)}, f32[640,320]{0,1:T(8,128)S(1)}, u32[]{:S(2)}, u32[]{:S(2)}) collective-permute-start(f32[640,320]{0,1:T(8,128)S(1)} %fusion.67), channel_id=1, source_target_pairs={{0,16},{8,24},{16,0},{24,8},{1,17},{9,25},{17,1},{25,9},{2,18},{10... | collective-permute-start | bytes 2457608 | tf_op jit(solution)/shard_map/ppermute | solution.py:111
  380.5 70.5 %collective-permute-start.22 = (f32[640,320]{0,1:T(8,128)S(1)}, f32[640,320]{0,1:T(8,128)S(1)}, u32[]{:S(2)}, u32[]{:S(2)}) collective-permute-start(f32[640,320]{0,1:T(8,128)S(1)} %fusion.63), channel_id=1, source_target_pairs={{0,24},{8,16},{16,8},{24,0},{1,25},{9,17},{17,9},{25,1},{2,26},{10... | collective-permute-start | bytes 2457608 | tf_op jit(solution)/shard_map/ppermute | solution.py:111
  380.9 76.3 %collective-permute-start.37 = (f32[640,320]{0,1:T(8,128)S(1)}, f32[640,320]{0,1:T(8,128)S(1)}, u32[]{:S(2)}, u32[]{:S(2)}) collective-permute-start(f32[640,320]{0,1:T(8,128)S(1)} %get-tuple-element.51), channel_id=1, source_target_pairs={{0,7},{1,0},{2,1},{3,2},{4,3},{5,4},{6,5},{7,6},{8,15},{9,8},{10,9... | collective-permute-start | bytes 2457608 | tf_op jit(solution)/shard_map/ppermute | solution.py:27
  396.4 62.3 %collective-permute-start.38 = (f32[640,320]{0,1:T(8,128)S(1)}, f32[640,320]{0,1:T(8,128)S(1)}, u32[]{:S(2)}, u32[]{:S(2)}) collective-permute-start(f32[640,320]{0,1:T(8,128)S(1)} %collective-permute-done.36), channel_id=1, source_target_pairs={{0,1},{1,2},{2,3},{3,4},{4,5},{5,6},{6,7},{7,0},{8,9},{9,10},{10,1... | collective-permute-start | bytes 2457608 | tf_op jit(solution)/shard_map/ppermute | solution.py:22
  458.7 38.3 %collective-permute-start.40 = (f32[640,320]{0,1:T(8,128)S(1)}, f32[640,320]{0,1:T(8,128)S(1)}, u32[]{:S(2)}, u32[]{:S(2)}) collective-permute-start(f32[640,320]{0,1:T(8,128)S(1)} %collective-permute-done.38), channel_id=1, source_target_pairs={{0,1},{1,2},{2,3},{3,4},{4,5},{5,6},{6,7},{7,0},{8,9},{9,10},{10,1... | collective-permute-start | bytes 2457608 | tf_op jit(solution)/shard_map/ppermute | solution.py:22
  537.6 50.0 %collective-permute-start.46 = (f16[656,320]{0,1:T(8,128)(2,1)}, f16[656,320]{0,1:T(8,128)(2,1)}, u32[]{:S(2)}, u32[]{:S(2)}) collective-permute-start(f16[656,320]{0,1:T(8,128)(2,1)} %pad_maximum_fusion), channel_id=1, source_target_pairs={{0,8},{8,0},{16,24},{24,16},{1,9},{9,1},{17,25},{25,17},{2,10},{10... | collective-permute-start | bytes 1259528 | tf_op jit(solution)/shard_map/ppermute | solution.py:111
  538.8 49.9 %collective-permute-start.47 = (f16[656,320]{0,1:T(8,128)(2,1)}, f16[656,320]{0,1:T(8,128)(2,1)}, u32[]{:S(2)}, u32[]{:S(2)}) collective-permute-start(f16[656,320]{0,1:T(8,128)(2,1)} %pad_maximum_fusion.1), channel_id=1, source_target_pairs={{0,16},{8,24},{16,0},{24,8},{1,17},{9,25},{17,1},{25,9},{2,18},{10... | collective-permute-start | bytes 1259528 | tf_op jit(solution)/shard_map/ppermute | solution.py:111
  541.0 49.1 %collective-permute-start.48 = (f16[656,320]{0,1:T(8,128)(2,1)}, f16[656,320]{0,1:T(8,128)(2,1)}, u32[]{:S(2)}, u32[]{:S(2)}) collective-permute-start(f16[656,320]{0,1:T(8,128)(2,1)} %pad_maximum_fusion.2), channel_id=1, source_target_pairs={{0,24},{8,16},{16,8},{24,0},{1,25},{9,17},{17,9},{25,1},{2,26},{10... | collective-permute-start | bytes 1259528 | tf_op jit(solution)/shard_map/ppermute | solution.py:111
  595.9 45.2 %collective-permute-start.51 = (f16[656,320]{0,1:T(8,128)(2,1)S(1)}, f16[656,320]{0,1:T(8,128)(2,1)S(1)}, u32[]{:S(2)}, u32[]{:S(2)}) collective-permute-start(f16[656,320]{0,1:T(8,128)(2,1)S(1)} %pad_maximum_fusion.3), channel_id=1, source_target_pairs={{0,24},{8,16},{16,8},{24,0},{1,25},{9,17},{17,9},{25,1},{2,26},{10... | collective-permute-start | bytes 1259528 | tf_op jit(solution)/shard_map/ppermute | solution.py:91
  599.8 42.9 %collective-permute-start.49 = (f16[656,320]{0,1:T(8,128)(2,1)S(1)}, f16[656,320]{0,1:T(8,128)(2,1)S(1)}, u32[]{:S(2)}, u32[]{:S(2)}) collective-permute-start(f16[656,320]{0,1:T(8,128)(2,1)S(1)} %pad_maximum_fusion.3), channel_id=1, source_target_pairs={{0,8},{8,0},{16,24},{24,16},{1,9},{9,1},{17,25},{25,17},{2,10},{10... | collective-permute-start | bytes 1259528 | tf_op jit(solution)/shard_map/ppermute | solution.py:91
  778.4 44.6 %collective-permute-start.61 = (f16[656,320]{0,1:T(8,128)(2,1)S(1)}, f16[656,320]{0,1:T(8,128)(2,1)S(1)}, u32[]{:S(2)}, u32[]{:S(2)}) collective-permute-start(f16[656,320]{0,1:T(8,128)(2,1)S(1)} %pad_maximum_fusion.6), channel_id=1, source_target_pairs={{0,24},{8,16},{16,8},{24,0},{1,25},{9,17},{17,9},{25,1},{2,26},{10... | collective-permute-start | bytes 1259528 | tf_op jit(solution)/shard_map/ppermute | solution.py:111
  826.6 43.9 %collective-permute-start.64 = (f16[656,320]{0,1:T(8,128)(2,1)S(1)}, f16[656,320]{0,1:T(8,128)(2,1)S(1)}, u32[]{:S(2)}, u32[]{:S(2)}) collective-permute-start(f16[656,320]{0,1:T(8,128)(2,1)S(1)} %pad_maximum_fusion.7), channel_id=1, source_target_pairs={{0,24},{8,16},{16,8},{24,0},{1,25},{9,17},{17,9},{25,1},{2,26},{10... | collective-permute-start | bytes 1259528 | tf_op jit(solution)/shard_map/ppermute | solution.py:91
  874.3 38.1 %collective-permute-start.66 = (f32[640,320]{0,1:T(8,128)S(1)}, f32[640,320]{0,1:T(8,128)S(1)}, u32[]{:S(2)}, u32[]{:S(2)}) collective-permute-start(f32[640,320]{0,1:T(8,128)S(1)} %get-tuple-element.71), channel_id=1, source_target_pairs={{0,7},{1,0},{2,1},{3,2},{4,3},{5,4},{6,5},{7,6},{8,15},{9,8},{10,9... | collective-permute-start | bytes 2457608 | tf_op jit(solution)/shard_map/ppermute | solution.py:27
  1006.2 42.4 %collective-permute-start.74 = (f16[656,320]{0,1:T(8,128)(2,1)S(1)}, f16[656,320]{0,1:T(8,128)(2,1)S(1)}, u32[]{:S(2)}, u32[]{:S(2)}) collective-permute-start(f16[656,320]{0,1:T(8,128)(2,1)S(1)} %pad_maximum_fusion.10), channel_id=1, source_target_pairs={{0,24},{8,16},{16,8},{24,0},{1,25},{9,17},{17,9},{25,1},{2,26},{10... | collective-permute-start | bytes 1259528 | tf_op jit(solution)/shard_map/ppermute | solution.py:111
  1053.1 41.0 %collective-permute-start.77 = (f16[656,320]{0,1:T(8,128)(2,1)S(1)}, f16[656,320]{0,1:T(8,128)(2,1)S(1)}, u32[]{:S(2)}, u32[]{:S(2)}) collective-permute-start(f16[656,320]{0,1:T(8,128)(2,1)S(1)} %pad_maximum_fusion.11), channel_id=1, source_target_pairs={{0,24},{8,16},{16,8},{24,0},{1,25},{9,17},{17,9},{25,1},{2,26},{10... | collective-permute-start | bytes 1259528 | tf_op jit(solution)/shard_map/ppermute | solution.py:91
  (73 other events, 2452.4 us)
